TPU v7x, 128 devices: a whole 4x4x4 slice. The times are simulated.
128 devices in a mesh: fsdp: 4 (over y_lo, core), ctx: 32 (over z, y_hi, x).
Axes of the slice: x: 4, y: 4 (y_hi: 2, y_lo: 2; y = y_hi * 2 + y_lo), z: 4, core: 2. Of those that a mesh axis runs over, the one named last changes fastest.
Arguments:
- query_proj: bfloat16 [4, 4096, 4096], P('fsdp', 'ctx'), may hold values from -10 to 10
- key_proj: bfloat16 [4, 4096, 4096], P('fsdp', 'ctx'), may hold values from -10 to 10
- value_proj: bfloat16 [4, 4096, 4096], P('fsdp', 'ctx'), may hold values from -12 to 12
- modality: int32 [4, 4096], P('fsdp', 'ctx'), may hold values from 0 to 1, as said below
- out_weight: bfloat16 [2, 4096, 2048], P(None, ('fsdp', 'ctx')), may hold values from -0.09375 to 0.09375
- grad_projected: bfloat16 [4, 4096, 2048], P('fsdp', 'ctx'), may hold values from -6 to 6
Outputs:
- projected: bfloat16 [4, 4096, 2048], P('fsdp', 'ctx')
- grad_query: bfloat16 [4, 4096, 4096], P('fsdp', 'ctx')
- grad_key: bfloat16 [4, 4096, 4096], P('fsdp', 'ctx')
- grad_value: bfloat16 [4, 4096, 4096], P('fsdp', 'ctx')
Inputs may be any that keep to these rules, and one draw needn't show every extreme that they name: `modality`: each sequence holds exactly two image spans of 1024 positions each, one starting within the first half and lying in the first half, the other lying in the second half; all other positions are text, so exactly half of each sequence's positions are image.
All inputs are finite; a program needn't handle non-finite values.
Results may differ from a plain program's by a relative error of at most 0.012.
The roundings to bfloat16 on the way count: a program that leaves them out, or rounds other values in their place, can miss the bound.
Values may be sent and summed in bfloat16 or wider, within the bound.
No kernel may reach another device: no remote copies, remote signals or barrier semaphores. Data moves between devices by JAX's collectives and lax.ppermute only.
A program may use at most 320 MiB of HBM per device.

v0:
```python
import jax
import jax.numpy as jnp
from jax import lax
from jax.sharding import PartitionSpec as P

HEAD_SIZE = 128


def cut_along(array, dim, length):
    before, after = (array.shape[:dim], array.shape[dim + 1 :])
    return jnp.moveaxis(array.reshape(*before, length, -1, *after), dim, 0)


def edges_of(length, count):
    unit = 8 if length >= 8 * count else 1
    return [length // unit * k // count * unit for k in range(1, count)]


def in_order(blocks, dim):
    dims = list(blocks.shape[1:])
    dims[dim] *= blocks.shape[0]
    return jnp.moveaxis(blocks, 0, dim).reshape(dims)


def exchange_in_pieces(array, axis, pieces, split_dim, concat_dim):
    blocks = cut_along(array, split_dim, lax.axis_size(axis))
    widest = max(range(1, max(2, blocks.ndim - 1)), key=lambda d: blocks.shape[d])
    done = []
    for share in jnp.split(blocks, edges_of(blocks.shape[widest], pieces), axis=widest):
        if share.size:
            done.append(lax.all_to_all(share, axis, split_axis=0, concat_axis=0, tiled=True))
    return in_order(jnp.concatenate(done, axis=widest), concat_dim)


def sent_together(arrays, axis, split_dim, concat_dim, along):
    widths = [a.shape[along] for a in arrays]
    both = jnp.concatenate(arrays, axis=along)
    filled = lax.all_to_all(both, axis, split_axis=split_dim, concat_axis=concat_dim, tiled=True)
    return tuple(jnp.split(filled, [sum(widths[:k]) for k in range(1, len(widths))], axis=along))


def block_count(length):
    return max(1, min(8, length // 512))


def probabilities(query_block, key_prefix, offset):
    scaling = query_block.shape[-1] ** (-0.5)
    scores = (
        jnp.einsum("hqd,hkd->hqk", query_block, key_prefix, preferred_element_type=jnp.float32)
        * scaling
    )
    query_places = offset + jnp.arange(query_block.shape[1])
    key_places = jnp.arange(key_prefix.shape[1])
    scores = jnp.where(key_places[None, None, :] <= query_places[None, :, None], scores, -jnp.inf)
    highest = jnp.max(scores, axis=-1, keepdims=True)
    raised = jnp.exp(scores - highest)
    return raised / jnp.sum(raised, axis=-1, keepdims=True)


def attend_forward(queries, keys_all, values_all):
    length = queries.shape[1]
    block_rows = length // block_count(length)
    pieces = []
    for block_index in range(length // block_rows):
        offset = block_index * block_rows
        finish = offset + block_rows
        weights = probabilities(queries[:, offset:finish], keys_all[:, :finish], offset).astype(
            jnp.bfloat16
        )
        output = jnp.einsum(
            "hqk,hkd->hqd", weights, values_all[:, :finish], preferred_element_type=jnp.float32
        )
        pieces.append(output.astype(jnp.bfloat16))
    return jnp.concatenate(pieces, axis=1)


def attend_backward(queries, keys_all, values_all, attention, grad_attention):
    length = queries.shape[1]
    block_rows = length // block_count(length)
    scaling = queries.shape[-1] ** (-0.5)
    grad_keys = jnp.zeros(queries.shape, jnp.float32)
    grad_values = jnp.zeros(queries.shape, jnp.float32)
    query_pieces = []
    for block_index in range(length // block_rows):
        offset = block_index * block_rows
        finish = offset + block_rows
        query_block = queries[:, offset:finish]
        weights = probabilities(query_block, keys_all[:, :finish], offset)
        grad_block = grad_attention[:, offset:finish]
        attn_block = attention[:, offset:finish]
        grad_values = grad_values.at[:, :finish].add(
            jnp.einsum(
                "hqk,hqd->hkd",
                weights.astype(jnp.bfloat16),
                grad_block,
                preferred_element_type=jnp.float32,
            )
        )
        grad_weights = jnp.einsum(
            "hqd,hkd->hqk", grad_block, values_all[:, :finish], preferred_element_type=jnp.float32
        )
        row_delta = jnp.sum(
            grad_block.astype(jnp.float32) * attn_block.astype(jnp.float32), axis=-1, keepdims=True
        )
        grad_scores = (weights * (grad_weights - row_delta) * scaling).astype(jnp.bfloat16)
        query_pieces.append(
            jnp.einsum(
                "hqk,hkd->hqd",
                grad_scores,
                keys_all[:, :finish],
                preferred_element_type=jnp.float32,
            ).astype(jnp.bfloat16)
        )
        grad_keys = grad_keys.at[:, :finish].add(
            jnp.einsum("hqk,hqd->hkd", grad_scores, query_block, preferred_element_type=jnp.float32)
        )
    return (
        jnp.concatenate(query_pieces, axis=1),
        grad_keys.astype(jnp.bfloat16),
        grad_values.astype(jnp.bfloat16),
    )


def transposed_product(left, right):
    return lax.dot_general(
        left, right, (((1,), (1,)), ((), ())), preferred_element_type=jnp.float32
    )


def heads_first(flat, length, local_heads):
    return flat.reshape(length, local_heads, HEAD_SIZE).transpose(1, 0, 2)


def heads_last(stacked, length, local_width):
    return stacked.transpose(1, 0, 2).reshape(1, length, local_width)


def per_device(query_proj, key_proj, value_proj, modality, out_weight, grad_projected):
    context_size = lax.axis_size("ctx")
    row_count = query_proj.shape[1]
    inner_width = query_proj.shape[2]
    length = row_count * context_size
    local_width = inner_width // context_size
    local_heads = local_width // HEAD_SIZE
    head_query, head_key, head_value = (
        exchange_in_pieces(query_proj, "ctx", 2, 2, 1),
        exchange_in_pieces(key_proj, "ctx", 2, 2, 1),
        exchange_in_pieces(value_proj, "ctx", 2, 2, 1),
    )
    head_query = heads_first(head_query, length, local_heads)
    head_key = heads_first(head_key, length, local_heads)
    head_value = heads_first(head_value, length, local_heads)
    attention = attend_forward(head_query, head_key, head_value)
    sending = heads_last(attention, length, local_width)
    attn_rows = lax.all_to_all(sending, "ctx", split_axis=1, concat_axis=2, tiled=True)[0]
    upstream = grad_projected[0]
    weight_piece = lax.all_gather(out_weight, ("fsdp", "ctx"), axis=1, tiled=True)
    text_out = jnp.dot(attn_rows, weight_piece[0], preferred_element_type=jnp.float32)
    image_out = jnp.dot(attn_rows, weight_piece[1], preferred_element_type=jnp.float32)
    text_grad = transposed_product(upstream, weight_piece[0])
    image_grad = transposed_product(upstream, weight_piece[1])
    text_out, image_out, text_grad, image_grad = (text_out, image_out, text_grad, image_grad)
    image_rows = (modality[0] == 1)[:, None]
    projected = jnp.where(image_rows, image_out, text_out).astype(jnp.bfloat16)[None]
    grad_rows = jnp.where(image_rows, image_grad, text_grad).astype(jnp.bfloat16)
    grad_heads = lax.all_to_all(grad_rows[None], "ctx", split_axis=2, concat_axis=1, tiled=True)
    grad_heads = heads_first(grad_heads, length, local_heads)
    grad_q, grad_k, grad_v = attend_backward(
        head_query, head_key, head_value, attention, grad_heads
    )
    grad_query, grad_key, grad_value = sent_together(
        (
            heads_last(grad_q, length, local_width),
            heads_last(grad_k, length, local_width),
            heads_last(grad_v, length, local_width),
        ),
        "ctx",
        1,
        2,
        0,
    )
    return (projected, grad_query, grad_key, grad_value)


def solution(mesh):
    placed = (
        P("fsdp", "ctx", None),
        P("fsdp", "ctx", None),
        P("fsdp", "ctx", None),
        P("fsdp", "ctx"),
        P(None, ("fsdp", "ctx"), None),
        P("fsdp", "ctx", None),
    )
    return jax.shard_map(
        per_device,
        mesh=mesh,
        in_specs=placed,
        out_specs=(
            P("fsdp", "ctx", None),
            P("fsdp", "ctx", None),
            P("fsdp", "ctx", None),
            P("fsdp", "ctx", None),
        ),
        check_vma=False,
    )
```

profile of v0, /device:TPU:18, one launch (start us, length us, event | category | flops | bytes accessed | tf_op | source)
XLA Modules:
  0.0 680.0 jit_solution(4088822224911274134)
XLA Ops:
  13.4 10.9 %all-to-all-start.3 = ((bf16[32,1,64,128]{3,2,1,0:T(8,128)(2,1)}), bf16[32,1,64,128]{3,2,1,0:T(8,128)(2,1)S(1)}, u32[]{:S(2)}, u32[]{:S(2)}) async-start(bf16[32,1,64,128]{3,2,1,0:T(8,128)(2,1)} %copy.65), calls=%async_computation.3 | async-start | bytes 1048576 | tf_op jit(solution)/shard_map/all_to_all | solution.py:31
  25.4 11.5 %all-to-all-done.3 = bf16[32,1,64,128]{3,2,1,0:T(8,128)(2,1)S(1)} async-done(((bf16[32,1,64,128]{3,2,1,0:T(8,128)(2,1)}), bf16[32,1,64,128]{3,2,1,0:T(8,128)(2,1)S(1)}, u32[]{:S(2)}, u32[]{:S(2)}) %all-to-all-start.3) | async-done | bytes 524320 | tf_op jit(solution)/shard_map/all_to_all | solution.py:31
  36.8 7.5 %all-to-all-start.2 = ((bf16[32,1,64,128]{3,2,1,0:T(8,128)(2,1)}), bf16[32,1,64,128]{3,2,1,0:T(8,128)(2,1)}, u32[]{:S(2)}, u32[]{:S(2)}) async-start(bf16[32,1,64,128]{3,2,1,0:T(8,128)(2,1)} %copy.64), calls=%async_computation.2 | async-start | bytes 1048576 | tf_op jit(solution)/shard_map/all_to_all | solution.py:31
  49.7 6.4 all-to-all-done.2
  56.1 7.5 %all-to-all-start.1 = ((bf16[32,1,64,128]{3,2,1,0:T(8,128)(2,1)}), bf16[32,1,64,128]{3,2,1,0:T(8,128)(2,1)S(1)}, u32[]{:S(2)}, u32[]{:S(2)}) async-start(bf16[32,1,64,128]{3,2,1,0:T(8,128)(2,1)} %copy.60), calls=%async_computation.1 | async-start | bytes 1048576 | tf_op jit(solution)/shard_map/all_to_all | solution.py:31
  64.8 10.1 %all-to-all-done.1 = bf16[32,1,64,128]{3,2,1,0:T(8,128)(2,1)S(1)} async-done(((bf16[32,1,64,128]{3,2,1,0:T(8,128)(2,1)}), bf16[32,1,64,128]{3,2,1,0:T(8,128)(2,1)S(1)}, u32[]{:S(2)}, u32[]{:S(2)}) %all-to-all-start.1) | async-done | bytes 524320 | tf_op jit(solution)/shard_map/all_to_all | solution.py:31
  75.7 7.6 %all-to-all-start = ((bf16[32,1,64,128]{3,2,1,0:T(8,128)(2,1)}), bf16[32,1,64,128]{3,2,1,0:T(8,128)(2,1)}, u32[]{:S(2)}, u32[]{:S(2)}) async-start(bf16[32,1,64,128]{3,2,1,0:T(8,128)(2,1)} %copy.59), calls=%async_computation | async-start | bytes 1048576 | tf_op jit(solution)/shard_map/all_to_all | solution.py:31
  92.8 7.9 %all-to-all-start.5 = ((bf16[32,1,64,128]{3,2,1,0:T(8,128)(2,1)}), bf16[32,1,64,128]{3,2,1,0:T(8,128)(2,1)S(1)}, u32[]{:S(2)}, u32[]{:S(2)}) async-start(bf16[32,1,64,128]{3,2,1,0:T(8,128)(2,1)} %copy.70), calls=%async_computation.5 | async-start | bytes 1048576 | tf_op jit(solution)/shard_map/all_to_all | solution.py:31
  100.7 9.6 %all-to-all-done.5 = bf16[32,1,64,128]{3,2,1,0:T(8,128)(2,1)S(1)} async-done(((bf16[32,1,64,128]{3,2,1,0:T(8,128)(2,1)}), bf16[32,1,64,128]{3,2,1,0:T(8,128)(2,1)S(1)}, u32[]{:S(2)}, u32[]{:S(2)}) %all-to-all-start.5) | async-done | bytes 524320 | tf_op jit(solution)/shard_map/all_to_all | solution.py:31
  110.3 8.3 %all-to-all-start.4 = ((bf16[32,1,64,128]{3,2,1,0:T(8,128)(2,1)}), bf16[32,1,64,128]{3,2,1,0:T(8,128)(2,1)}, u32[]{:S(2)}, u32[]{:S(2)}) async-start(bf16[32,1,64,128]{3,2,1,0:T(8,128)(2,1)} %copy.69), calls=%async_computation.4 | async-start | bytes 1048576 | tf_op jit(solution)/shard_map/all_to_all | solution.py:31
  121.8 6.5 all-to-all-done.4
  169.4 211.5 %all-gather.2.cloned.1.call-done = bf16[2,4096,2048]{2,1,0:T(8,128)(2,1)} async-done(((bf16[2,32,2048]{2,1,0:T(8,128)(2,1)}), bf16[2,4096,2048]{2,1,0:T(8,128)(2,1)}) %all-gather.2.cloned.1.call-update) | async-done | bytes 33554448 | tf_op jit(solution)/shard_map/all_gather | solution.py:157
  380.8 12.4 %fusion = bf16[128,4096]{1,0:T(8,128)(2,1)} fusion(bf16[2,4096,2048]{2,1,0:T(8,128)(2,1)} %all-gather.2.cloned.1.call-done, bf16[1,128,2048]{2,1,0:T(8,128)(2,1)S(1)} %copy-done), kind=kOutput, calls=%fused_computation.2 | convolution fusion | flops 2147483648 | bytes 18350080 | tf_op jit(solution)/shard_map/dot_general | solution.py:125
  393.2 11.6 %fusion.20 = bf16[1,128,4096]{2,1,0:T(8,128)(2,1)S(1)} fusion(bf16[128,4096]{1,0:T(8,128)(2,1)} %fusion, bf16[2,4096,2048]{2,1,0:T(8,128)(2,1)} %all-gather.2.cloned.1.call-done, pred[128]{0:T(512)(128)(4,1)S(1)} %compare_bitcast_fusion, bf16[1,128,2048]{2,1,0:T(8,128)(2,1)S(1)} %copy-done), kind=kOutput, calls=%fused_computation.42 | convolution fusion | flops 2148007936 | bytes 19398784 | tf_op jit(solution)/shard_map/dot_general | solution.py:125
  409.3 23.6 %reduce.73 = bf16[4096,128]{1,0:T(8,128)(2,1)S(1)} reduce(bf16[4096,1,128]{2,1,0:T(2,128)(2,1)} %bitcast.454, bf16[]{:T(256)} %broadcast.495), dimensions={1}, to_apply=%bitcast.334.reduce_sub_computation | reduce | bytes 2097154
  434.0 10.3 %all-to-all-start.7 = ((bf16[32,2,8192]{2,1,0:T(2,128)(2,1)}), bf16[32,2,8192]{2,1,0:T(2,128)(2,1)S(1)}, u32[]{:S(2)}, u32[]{:S(2)}) async-start(bf16[32,2,8192]{2,1,0:T(2,128)(2,1)} %reshape.1112), calls=%async_computation.7 | async-start | bytes 2097152 | tf_op jit(solution)/shard_map/all_to_all | solution.py:166
  460.2 24.4 %reduce.72 = bf16[4096,128]{1,0:T(8,128)(2,1)} reduce(bf16[4096,1,128]{2,1,0:T(2,128)(2,1)} %bitcast.455, bf16[]{:T(256)} %broadcast.495), dimensions={1}, to_apply=%bitcast.405.reduce_sub_computation | reduce | bytes 2097154
  486.7 9.9 %all-to-all-start.6 = ((bf16[32,2,8192]{2,1,0:T(2,128)(2,1)}), bf16[32,2,8192]{2,1,0:T(2,128)(2,1)}, u32[]{:S(2)}, u32[]{:S(2)}) async-start(bf16[32,2,8192]{2,1,0:T(2,128)(2,1)} %reshape.1110), calls=%async_computation.6 | async-start | bytes 2097152 | tf_op jit(solution)/shard_map/all_to_all | solution.py:155
  556.1 20.5 %copy.78 = bf16[3,4096,128]{2,0,1:T(4,128)(2,1)} copy(bf16[3,4096,128]{2,1,0:T(8,128)(2,1)S(1)} %pad_maximum_fusion) | data formatting | bytes 6291456 | tf_op jit(solution)/shard_map/concatenate | solution.py:37
  576.6 10.3 %all-to-all-start.8 = ((bf16[3,4096,128]{2,0,1:T(4,128)(2,1)}), bf16[3,4096,128]{2,0,1:T(4,128)(2,1)}, u32[]{:S(2)}, u32[]{:S(2)}) async-start(bf16[3,4096,128]{2,0,1:T(4,128)(2,1)} %copy.78), calls=%async_computation.8 | async-start | bytes 8388608 | tf_op jit(solution)/shard_map/all_to_all | solution.py:38
  593.9 8.1 %fusion.1 = bf16[128,2048]{1,0:T(8,128)(2,1)S(1)} fusion(bf16[128,4096]{0,1:T(8,128)(2,1)S(1)} %bitcast.493, bf16[2,4096,2048]{2,1,0:T(8,128)(2,1)} %all-gather.2.cloned.1.call-done), kind=kOutput, calls=%fused_computation.3 | convolution fusion | flops 2147483648 | bytes 18350080 | tf_op jit(solution)/shard_map/dot_general | solution.py:159
  602.1 8.9 %fusion.49 = bf16[1,128,2048]{2,1,0:T(8,128)(2,1)} fusion(bf16[128,2048]{1,0:T(8,128)(2,1)S(1)} %fusion.1, bf16[128,4096]{0,1:T(8,128)(2,1)S(1)} %bitcast.494, bf16[2,4096,2048]{2,1,0:T(8,128)(2,1)} %all-gather.2.cloned.1.call-done, pred[128]{0:T(512)(128)(4,1)S(1)} %copy-done.29), kind=kOutput, calls=%fused_computation.88 | convolution fusion | flops 2147745792 | bytes 18874496 | tf_op jit(solution)/shard_map/dot_general | solution.py:158
  611.0 35.8 %all-to-all-done.8 = bf16[3,4096,128]{2,0,1:T(4,128)(2,1)} async-done(((bf16[3,4096,128]{2,0,1:T(4,128)(2,1)}), bf16[3,4096,128]{2,0,1:T(4,128)(2,1)}, u32[]{:S(2)}, u32[]{:S(2)}) %all-to-all-start.8) | async-done | bytes 3145760 | tf_op jit(solution)/shard_map/all_to_all | solution.py:38
  646.7 10.9 %fusion.163 = (bf16[1,128,32,128]{3,0,1,2:T(2,128)(2,1)S(1)}, bf16[1,128,32,128]{3,0,1,2:T(2,128)(2,1)}, bf16[1,128,32,128]{3,0,1,2:T(2,128)(2,1)S(1)}) fusion(bf16[3,128,32,128]{3,0,1,2:T(4,128)(2,1)} %bitcast.93), kind=kLoop, calls=%fused_computation.257 | loop fusion | bytes 6291456 | tf_op jit(solution)/shard_map/split | solution.py:39
  (196 shorter events, 173.0 us)
Async XLA Ops:
  7.2 373.7 %copy-start = (bf16[1,128,2048]{2,1,0:T(8,128)(2,1)S(1)}, bf16[1,128,2048]{2,1,0:T(8,128)(2,1)}, u32[]{:S(2)}) copy-start(bf16[1,128,2048]{2,1,0:T(8,128)(2,1)} %param.47) | copy-start | bytes 1572868
  7.2 373.7 %all-gather.2.cloned.1.call-start = ((), (), s32[]{:S(2)}) async-start(), calls=%async_computation.9 | async-start | bytes 33816576 | tf_op jit(solution)/shard_map/all_gather | solution.py:157
  13.4 23.5 %all-to-all-start.3 = ((bf16[32,1,64,128]{3,2,1,0:T(8,128)(2,1)}), bf16[32,1,64,128]{3,2,1,0:T(8,128)(2,1)S(1)}, u32[]{:S(2)}, u32[]{:S(2)}) async-start(bf16[32,1,64,128]{3,2,1,0:T(8,128)(2,1)} %copy.65), calls=%async_computation.3 | async-start | bytes 1048576 | tf_op jit(solution)/shard_map/all_to_all | solution.py:31
  36.8 19.3 %all-to-all-start.2 = ((bf16[32,1,64,128]{3,2,1,0:T(8,128)(2,1)}), bf16[32,1,64,128]{3,2,1,0:T(8,128)(2,1)}, u32[]{:S(2)}, u32[]{:S(2)}) async-start(bf16[32,1,64,128]{3,2,1,0:T(8,128)(2,1)} %copy.64), calls=%async_computation.2 | async-start | bytes 1048576 | tf_op jit(solution)/shard_map/all_to_all | solution.py:31
  56.1 18.8 %all-to-all-start.1 = ((bf16[32,1,64,128]{3,2,1,0:T(8,128)(2,1)}), bf16[32,1,64,128]{3,2,1,0:T(8,128)(2,1)S(1)}, u32[]{:S(2)}, u32[]{:S(2)}) async-start(bf16[32,1,64,128]{3,2,1,0:T(8,128)(2,1)} %copy.60), calls=%async_computation.1 | async-start | bytes 1048576 | tf_op jit(solution)/shard_map/all_to_all | solution.py:31
  75.7 17.1 %all-to-all-start = ((bf16[32,1,64,128]{3,2,1,0:T(8,128)(2,1)}), bf16[32,1,64,128]{3,2,1,0:T(8,128)(2,1)}, u32[]{:S(2)}, u32[]{:S(2)}) async-start(bf16[32,1,64,128]{3,2,1,0:T(8,128)(2,1)} %copy.59), calls=%async_computation | async-start | bytes 1048576 | tf_op jit(solution)/shard_map/all_to_all | solution.py:31
  86.4 32.1 %copy-start.27 = (s32[1,128]{1,0:T(1,128)S(1)}, s32[1,128]{1,0:T(1,128)}, u32[]{:S(2)}) copy-start(s32[1,128]{1,0:T(1,128)} %param.45) | copy-start | bytes 1540
  88.8 31.9 %copy-start.15 = (bf16[32,1,64,128]{3,2,1,0:T(8,128)(2,1)S(1)}, bf16[32,1,64,128]{3,2,1,0:T(8,128)(2,1)}, u32[]{:S(2)}) copy-start(bf16[32,1,64,128]{3,2,1,0:T(8,128)(2,1)} %copy-done.14) | copy-start | bytes 1572868
  92.8 17.5 %all-to-all-start.5 = ((bf16[32,1,64,128]{3,2,1,0:T(8,128)(2,1)}), bf16[32,1,64,128]{3,2,1,0:T(8,128)(2,1)S(1)}, u32[]{:S(2)}, u32[]{:S(2)}) async-start(bf16[32,1,64,128]{3,2,1,0:T(8,128)(2,1)} %copy.70), calls=%async_computation.5 | async-start | bytes 1048576 | tf_op jit(solution)/shard_map/all_to_all | solution.py:31
  110.3 18.1 %copy-start.16 = (bf16[32,1,64,128]{3,2,1,0:T(8,128)(2,1)}, bf16[32,1,64,128]{3,2,1,0:T(8,128)(2,1)S(1)}, u32[]{:S(2)}) copy-start(bf16[32,1,64,128]{3,2,1,0:T(8,128)(2,1)S(1)} %all-to-all-done.5) | copy-start | bytes 1572868
  110.3 18.1 %all-to-all-start.4 = ((bf16[32,1,64,128]{3,2,1,0:T(8,128)(2,1)}), bf16[32,1,64,128]{3,2,1,0:T(8,128)(2,1)}, u32[]{:S(2)}, u32[]{:S(2)}) async-start(bf16[32,1,64,128]{3,2,1,0:T(8,128)(2,1)} %copy.69), calls=%async_computation.4 | async-start | bytes 1048576 | tf_op jit(solution)/shard_map/all_to_all | solution.py:31
  118.6 274.7 %copy-start.28 = (pred[128]{0:T(512)(128)(4,1)}, pred[128]{0:T(512)(128)(4,1)S(1)}, u32[]{:S(2)}) copy-start(pred[128]{0:T(512)(128)(4,1)S(1)} %compare_bitcast_fusion) | copy-start | bytes 388
  121.8 32.1 %copy-start.7 = (bf16[32,1,128,128]{3,2,0,1:T(8,128)(2,1)}, bf16[32,1,128,128]{3,2,0,1:T(8,128)(2,1)S(1)}, u32[]{:S(2)}) copy-start(bf16[32,1,128,128]{3,2,0,1:T(8,128)(2,1)S(1)} %pad_maximum_fusion.1) | copy-start | bytes 3145732
  132.8 6.1 copy-start.12
  132.8 6.1 copy-start.23
  133.3 5.6 copy-start.25
  134.6 5.5 copy-start.10
  434.0 52.7 %all-to-all-start.7 = ((bf16[32,2,8192]{2,1,0:T(2,128)(2,1)}), bf16[32,2,8192]{2,1,0:T(2,128)(2,1)S(1)}, u32[]{:S(2)}, u32[]{:S(2)}) async-start(bf16[32,2,8192]{2,1,0:T(2,128)(2,1)} %reshape.1112), calls=%async_computation.7 | async-start | bytes 2097152 | tf_op jit(solution)/shard_map/all_to_all | solution.py:166
  444.3 9.6 %slice-start = ((s8[8388608]{0:T(1024)(128)(4,1)}), s8[4194304]{0:T(1024)(128)(4,1)S(1)}, s32[]{:S(2)}) async-start(s8[8388608]{0:T(1024)(128)(4,1)} %bitcast.406), calls=%async_computation.10 | async-start | bytes 8388608
  486.7 89.9 %all-to-all-start.6 = ((bf16[32,2,8192]{2,1,0:T(2,128)(2,1)}), bf16[32,2,8192]{2,1,0:T(2,128)(2,1)}, u32[]{:S(2)}, u32[]{:S(2)}) async-start(bf16[32,2,8192]{2,1,0:T(2,128)(2,1)} %reshape.1110), calls=%async_computation.6 | async-start | bytes 2097152 | tf_op jit(solution)/shard_map/all_to_all | solution.py:155
  511.0 5.2 slice-start.8
  576.6 70.2 %all-to-all-start.8 = ((bf16[3,4096,128]{2,0,1:T(4,128)(2,1)}), bf16[3,4096,128]{2,0,1:T(4,128)(2,1)}, u32[]{:S(2)}, u32[]{:S(2)}) async-start(bf16[3,4096,128]{2,0,1:T(4,128)(2,1)} %copy.78), calls=%async_computation.8 | async-start | bytes 8388608 | tf_op jit(solution)/shard_map/all_to_all | solution.py:38
  593.9 8.1 %copy-start.29 = (pred[128]{0:T(512)(128)(4,1)S(1)}, pred[128]{0:T(512)(128)(4,1)}, u32[]{:S(2)}) copy-start(pred[128]{0:T(512)(128)(4,1)} %copy-done.28) | copy-start | bytes 388
  665.9 6.8 %copy-start.1 = (bf16[1,128,2048]{2,1,0:T(8,128)(2,1)S(1)}, bf16[1,128,2048]{2,1,0:T(8,128)(2,1)}, u32[]{:S(2)}) copy-start(bf16[1,128,2048]{2,1,0:T(8,128)(2,1)} %param.47) | copy-start | bytes 1572868
  (26 other events, 66.2 us)
Sparse Core Ops, SparseCore 0:
  9.7 371.0 all-gather.1
where the time goes:
time: 687 us; the launch traced here: 680 us
  waiting for transfers between devices  295 us (43%)
  matrix products  112 us (16%)
  local copies, waits for them, and re-layouts  102 us (15%)
  starting transfers between devices  80 us (12%)
  other arithmetic  76.6 us (11%)
  between operations  15.2 us (2%)
    all_gather x1, waiting for transfers between devices, per_device(): lax.all_gather(out_weight, ('fsdp', 'ctx'), axis=1, tiled=True)  211 us
    all_to_all x6, starting transfers between devices, exchange_in_pieces(): lax.all_to_all(share, axis, split_axis=0, concat_axis=0, tiled=True)  49.5 us
    unnamed x7, other arithmetic  48 us
    all_to_all x6, waiting for transfers between devices, exchange_in_pieces(): lax.all_to_all(share, axis, split_axis=0, concat_axis=0, tiled=True)  46.9 us
    all_to_all x1, waiting for transfers between devices, sent_together(): lax.all_to_all(both, axis, split_axis=split_dim, concat_axis=concat_dim,...  35.8 us
    unnamed x90, local copies, waits for them, and re-layouts  28.1 us
    split x7, local copies, waits for them, and re-layouts, sent_together(): jnp.split(filled, [sum(widths[:k]) for k in range(1, len(widths))], axis=...  26 us
    dot_general x2, matrix products, transposed_product(): lax.dot_general(left, right, (((1,), (1,)), ((), ())), preferred_element_...  24 us
  transfers between devices with their start and end apart: 10, of which 8 were waited for; matrix products, arithmetic and copies ran while one was open for 30% of the time, Pallas kernels for 0%

commit v1 on v0

--- a/solution.py
+++ b/solution.py
@@ -4,6 +4,13 @@
 from jax.sharding import PartitionSpec as P
 
 HEAD_SIZE = 128
+
+
+def gather_over(x, mesh_axis, along):
+    count = lax.axis_size(mesh_axis)
+    blocks = jnp.stack([x for _ in range(count)])
+    blocks = lax.all_to_all(blocks, mesh_axis, split_axis=0, concat_axis=0)
+    return jnp.concatenate(blocks, axis=along)
 
 
 def cut_along(array, dim, length):
@@ -154,7 +161,7 @@
     sending = heads_last(attention, length, local_width)
     attn_rows = lax.all_to_all(sending, "ctx", split_axis=1, concat_axis=2, tiled=True)[0]
     upstream = grad_projected[0]
-    weight_piece = lax.all_gather(out_weight, ("fsdp", "ctx"), axis=1, tiled=True)
+    weight_piece = gather_over(out_weight, ("fsdp", "ctx"), 1)
     text_out = jnp.dot(attn_rows, weight_piece[0], preferred_element_type=jnp.float32)
     image_out = jnp.dot(attn_rows, weight_piece[1], preferred_element_type=jnp.float32)
     text_grad = transposed_product(upstream, weight_piece[0])

time: 687 us -> 1020 us (1.48)
  waiting for transfers between devices: 295 us -> 563 us
  local copies, waits for them, and re-layouts: 102 us -> 137 us
  starting transfers between devices: 80 us -> 103 us
  blocking collectives: 0 us -> 15.8 us
  between operations: 15.2 us -> 1.87 us
    all_to_all x0 -> x1, waiting for transfers between devices: none -> 496 us  [gather_over(): blocks = lax.all_to_all(blocks, mesh_axis, split_axis=0, concat_axis=0)]
    all_gather x1 -> x0, waiting for transfers between devices: 211 us -> none  [per_device(): lax.all_gather(out_weight, ('fsdp', 'ctx'), axis=1, tiled=True)]
    slice x0 -> x1, local copies, waits for them, and re-layouts: none -> 23.8 us  [per_device(): weight_piece[0]]
    all_to_all x1, starting transfers between devices: 10.3 us -> 32.8 us  [per_device(): lax.all_to_all(grad_rows[None], 'ctx', split_axis=2, concat_axis=1, tiled...]
    all_to_all x6 -> x5, waiting for transfers between devices: 46.9 us -> 30.2 us  [exchange_in_pieces(): lax.all_to_all(share, axis, split_axis=0, concat_axis=0, tiled=True)]
    all_to_all x0 -> x1, blocking collectives: none -> 15.8 us  [exchange_in_pieces(): lax.all_to_all(share, axis, split_axis=0, concat_axis=0, tiled=True)]
    another operation x0 -> x1, local copies, waits for them, and re-layouts: none -> 11 us  [gather_over(): blocks = jnp.stack([x for _ in range(count)])]
    all_to_all x6 -> x5, starting transfers between devices: 49.5 us -> 41.4 us  [exchange_in_pieces(): lax.all_to_all(share, axis, split_axis=0, concat_axis=0, tiled=True)]
  transfers between devices with their start and end apart: 10 -> 9, of which waited for: 8 -> 7; matrix products, arithmetic and copies ran while one was open for 30% -> 20% of each run, Pallas kernels for 0% -> 0%
where the time goes in v1:
time: 1020 us; the launch traced here: 1010 us
  waiting for transfers between devices  563 us (55%)
  local copies, waits for them, and re-layouts  137 us (13%)
  matrix products  118 us (12%)
  starting transfers between devices  103 us (10%)
  other arithmetic  74.4 us (7%)
  blocking collectives  15.8 us (2%)
    all_to_all x1, waiting for transfers between devices, gather_over(): blocks = lax.all_to_all(blocks, mesh_axis, split_axis=0, concat_axis=0)  496 us
    unnamed x7, other arithmetic  47.8 us
    all_to_all x5, starting transfers between devices, exchange_in_pieces(): lax.all_to_all(share, axis, split_axis=0, concat_axis=0, tiled=True)  41.4 us
    all_to_all x1, waiting for transfers between devices, sent_together(): lax.all_to_all(both, axis, split_axis=split_dim, concat_axis=concat_dim,...  36.6 us
    all_to_all x1, starting transfers between devices, per_device(): lax.all_to_all(grad_rows[None], 'ctx', split_axis=2, concat_axis=1, tiled...  32.8 us
    all_to_all x5, waiting for transfers between devices, exchange_in_pieces(): lax.all_to_all(share, axis, split_axis=0, concat_axis=0, tiled=True)  30.2 us
    unnamed x104, local copies, waits for them, and re-layouts  28.2 us
    split x7, local copies, waits for them, and re-layouts, sent_together(): jnp.split(filled, [sum(widths[:k]) for k in range(1, len(widths))], axis=...  26 us
  transfers between devices with their start and end apart: 9, of which 7 were waited for; matrix products, arithmetic and copies ran while one was open for 20% of the time, Pallas kernels for 0%

profile of v1, /device:TPU:18, one launch (start us, length us, event | category | flops | bytes accessed | tf_op | source)
XLA Modules:
  0.0 1013.5 jit_solution(1876662461089046674)
XLA Ops:
  6.1 10.9 %all-to-all-start = ((bf16[32,1,64,128]{3,2,1,0:T(8,128)(2,1)}), bf16[32,1,64,128]{3,2,1,0:T(8,128)(2,1)S(1)}, u32[]{:S(2)}, u32[]{:S(2)}) async-start(bf16[32,1,64,128]{3,2,1,0:T(8,128)(2,1)} %copy.59), calls=%async_computation | async-start | bytes 1048576 | tf_op jit(solution)/shard_map/all_to_all | solution.py:38
  18.1 8.7 all-to-all-done
  26.8 7.8 all-to-all-start.1
  43.1 7.5 all-to-all-start.2
  59.8 7.8 all-to-all-start.3
  76.1 7.5 all-to-all-start.4
  84.0 8.0 all-to-all-done.4
  92.0 15.8 %all_to_all.83 = bf16[32,1,64,128]{3,2,1,0:T(8,128)(2,1)} all-to-all(bf16[32,1,64,128]{3,2,1,0:T(8,128)(2,1)S(1)} %copy.70), channel_id=1, replica_groups=mesh['fsdp'=4,'ctx'=32] {'ctx'}, dimensions={0} | all-to-all | bytes 1048576 | tf_op jit(solution)/shard_map/all_to_all | solution.py:38
  107.8 11.0 %stack.2 = bf16[128,2,32,2048]{3,2,1,0:T(8,128)(2,1)} broadcast(bf16[2,32,2048]{2,1,0:T(8,128)(2,1)S(1)} %copy-done.29), dimensions={1,2,3} | broadcast | bytes 33816576 | tf_op jit(solution)/shard_map/stack | solution.py:11
  118.8 8.9 all-to-all-start.7
  167.4 495.9 %all-to-all-done.7 = bf16[128,2,32,2048]{3,2,1,0:T(8,128)(2,1)} async-done(((bf16[128,2,32,2048]{3,2,1,0:T(8,128)(2,1)}), bf16[128,2,32,2048]{3,2,1,0:T(8,128)(2,1)}, u32[]{:S(2)}, u32[]{:S(2)}) %all-to-all-start.7) | async-done | bytes 33554464 | tf_op jit(solution)/shard_map/all_to_all | solution.py:12
  663.3 23.8 %fusion.158 = (bf16[1,128,32,2048]{3,2,0,1:T(8,128)(2,1)}, bf16[1,128,32,2048]{3,2,0,1:T(8,128)(2,1)}) fusion(bf16[2,128,32,2048]{3,2,0,1:T(8,128)(2,1)} %bitcast.53), kind=kLoop, calls=%fused_computation.252 | loop fusion | bytes 67108864 | tf_op jit(solution)/shard_map/slice | solution.py:165
  687.1 11.4 %fusion.117 = bf16[128,4096]{1,0:T(8,128)(2,1)S(1)} fusion(bf16[4096,2048]{1,0:T(8,128)(2,1)} %bitcast.393, bf16[1,128,2048]{2,1,0:T(8,128)(2,1)S(1)} %copy-done), kind=kOutput, calls=%fused_computation.177 | convolution fusion | flops 2147483648 | bytes 18350080 | tf_op jit(solution)/shard_map/dot_general | solution.py:132
  698.5 12.3 %fusion.15 = bf16[1,128,4096]{2,1,0:T(8,128)(2,1)} fusion(bf16[128,4096]{1,0:T(8,128)(2,1)S(1)} %fusion.117, bf16[4096,2048]{1,0:T(8,128)(2,1)} %bitcast.395, pred[128]{0:T(512)(128)(4,1)} %compare_bitcast_fusion, bf16[1,128,2048]{2,1,0:T(8,128)(2,1)S(1)} %copy-done), kind=kOutput, calls=%fused_computation.36 | convolution fusion | flops 2148007936 | bytes 19398784 | tf_op jit(solution)/shard_map/dot_general | solution.py:132
  716.9 23.4 %reduce.73 = bf16[4096,128]{1,0:T(8,128)(2,1)S(1)} reduce(bf16[4096,1,128]{2,1,0:T(2,128)(2,1)} %bitcast.447, bf16[]{:T(256)} %broadcast.497), dimensions={1}, to_apply=%bitcast.317.reduce_sub_computation | reduce | bytes 2097154
  741.4 32.8 %all-to-all-start.8 = ((bf16[32,2,8192]{2,1,0:T(2,128)(2,1)}), bf16[32,2,8192]{2,1,0:T(2,128)(2,1)S(1)}, u32[]{:S(2)}, u32[]{:S(2)}) async-start(bf16[32,2,8192]{2,1,0:T(2,128)(2,1)} %reshape.1123), calls=%async_computation.8 | async-start | bytes 2097152 | tf_op jit(solution)/shard_map/all_to_all | solution.py:173
  790.1 24.4 %reduce.72 = bf16[4096,128]{1,0:T(8,128)(2,1)} reduce(bf16[4096,1,128]{2,1,0:T(2,128)(2,1)} %bitcast.448, bf16[]{:T(256)} %broadcast.497), dimensions={1}, to_apply=%bitcast.392.reduce_sub_computation | reduce | bytes 2097154
  816.6 9.9 all-to-all-start.6
  895.4 20.5 %copy.78 = bf16[3,4096,128]{2,0,1:T(4,128)(2,1)} copy(bf16[3,4096,128]{2,1,0:T(8,128)(2,1)S(1)} %pad_maximum_fusion) | data formatting | bytes 6291456 | tf_op jit(solution)/shard_map/concatenate | solution.py:44
  916.0 10.3 %all-to-all-start.9 = ((bf16[3,4096,128]{2,0,1:T(4,128)(2,1)}), bf16[3,4096,128]{2,0,1:T(4,128)(2,1)}, u32[]{:S(2)}, u32[]{:S(2)}) async-start(bf16[3,4096,128]{2,0,1:T(4,128)(2,1)} %copy.78), calls=%async_computation.9 | async-start | bytes 8388608 | tf_op jit(solution)/shard_map/all_to_all | solution.py:45
  933.3 8.1 fusion.171
  941.4 8.9 fusion.43
  950.4 36.6 %all-to-all-done.9 = bf16[3,4096,128]{2,0,1:T(4,128)(2,1)} async-done(((bf16[3,4096,128]{2,0,1:T(4,128)(2,1)}), bf16[3,4096,128]{2,0,1:T(4,128)(2,1)}, u32[]{:S(2)}, u32[]{:S(2)}) %all-to-all-start.9) | async-done | bytes 3145760 | tf_op jit(solution)/shard_map/all_to_all | solution.py:45
  987.0 10.9 %fusion.159 = (bf16[1,128,32,128]{3,0,1,2:T(2,128)(2,1)S(1)}, bf16[1,128,32,128]{3,0,1,2:T(2,128)(2,1)}, bf16[1,128,32,128]{3,0,1,2:T(2,128)(2,1)S(1)}) fusion(bf16[3,128,32,128]{3,0,1,2:T(4,128)(2,1)} %bitcast.94), kind=kLoop, calls=%fused_computation.253 | loop fusion | bytes 6291456 | tf_op jit(solution)/shard_map/split | solution.py:46
  (210 shorter events, 188.5 us)
Async XLA Ops:
  0.6 686.5 %copy-start = (bf16[1,128,2048]{2,1,0:T(8,128)(2,1)S(1)}, bf16[1,128,2048]{2,1,0:T(8,128)(2,1)}, u32[]{:S(2)}) copy-start(bf16[1,128,2048]{2,1,0:T(8,128)(2,1)} %param.47) | copy-start | bytes 1572868
  6.1 20.7 %all-to-all-start = ((bf16[32,1,64,128]{3,2,1,0:T(8,128)(2,1)}), bf16[32,1,64,128]{3,2,1,0:T(8,128)(2,1)S(1)}, u32[]{:S(2)}, u32[]{:S(2)}) async-start(bf16[32,1,64,128]{3,2,1,0:T(8,128)(2,1)} %copy.59), calls=%async_computation | async-start | bytes 1048576 | tf_op jit(solution)/shard_map/all_to_all | solution.py:38
  26.8 16.4 %all-to-all-start.1 = ((bf16[32,1,64,128]{3,2,1,0:T(8,128)(2,1)}), bf16[32,1,64,128]{3,2,1,0:T(8,128)(2,1)}, u32[]{:S(2)}, u32[]{:S(2)}) async-start(bf16[32,1,64,128]{3,2,1,0:T(8,128)(2,1)} %copy.60), calls=%async_computation.1 | async-start | bytes 1048576 | tf_op jit(solution)/shard_map/all_to_all | solution.py:38
  43.1 15.9 %all-to-all-start.2 = ((bf16[32,1,64,128]{3,2,1,0:T(8,128)(2,1)}), bf16[32,1,64,128]{3,2,1,0:T(8,128)(2,1)S(1)}, u32[]{:S(2)}, u32[]{:S(2)}) async-start(bf16[32,1,64,128]{3,2,1,0:T(8,128)(2,1)} %copy.64), calls=%async_computation.2 | async-start | bytes 1048576 | tf_op jit(solution)/shard_map/all_to_all | solution.py:38
  59.8 16.3 %all-to-all-start.3 = ((bf16[32,1,64,128]{3,2,1,0:T(8,128)(2,1)}), bf16[32,1,64,128]{3,2,1,0:T(8,128)(2,1)}, u32[]{:S(2)}, u32[]{:S(2)}) async-start(bf16[32,1,64,128]{3,2,1,0:T(8,128)(2,1)} %copy.65), calls=%async_computation.3 | async-start | bytes 1048576 | tf_op jit(solution)/shard_map/all_to_all | solution.py:38
  70.6 37.2 %copy-start.29 = (bf16[2,32,2048]{2,1,0:T(8,128)(2,1)S(1)}, bf16[2,32,2048]{2,1,0:T(8,128)(2,1)}, u32[]{:S(2)}) copy-start(bf16[2,32,2048]{2,1,0:T(8,128)(2,1)} %param.46) | copy-start | bytes 786436
  76.1 15.9 %all-to-all-start.4 = ((bf16[32,1,64,128]{3,2,1,0:T(8,128)(2,1)}), bf16[32,1,64,128]{3,2,1,0:T(8,128)(2,1)S(1)}, u32[]{:S(2)}, u32[]{:S(2)}) async-start(bf16[32,1,64,128]{3,2,1,0:T(8,128)(2,1)} %copy.69), calls=%async_computation.4 | async-start | bytes 1048576 | tf_op jit(solution)/shard_map/all_to_all | solution.py:38
  92.0 26.8 %copy-start.21 = (bf16[32,1,64,128]{3,2,1,0:T(8,128)(2,1)}, bf16[32,1,64,128]{3,2,1,0:T(8,128)(2,1)S(1)}, u32[]{:S(2)}) copy-start(bf16[32,1,64,128]{3,2,1,0:T(8,128)(2,1)S(1)} %all-to-all-done.4) | copy-start | bytes 1572868
  118.8 9.0 copy-start.36
  118.8 10.7 %copy-start.20 = (bf16[32,1,64,128]{3,2,1,0:T(8,128)(2,1)S(1)}, bf16[32,1,64,128]{3,2,1,0:T(8,128)(2,1)}, u32[]{:S(2)}) copy-start(bf16[32,1,64,128]{3,2,1,0:T(8,128)(2,1)} %copy-done.19) | copy-start | bytes 1572868
  118.8 544.5 %all-to-all-start.7 = ((bf16[128,2,32,2048]{3,2,1,0:T(8,128)(2,1)}), bf16[128,2,32,2048]{3,2,1,0:T(8,128)(2,1)}, u32[]{:S(2)}, u32[]{:S(2)}) async-start(bf16[128,2,32,2048]{3,2,1,0:T(8,128)(2,1)} %stack.2), calls=%async_computation.7 | async-start | bytes 67108864 | tf_op jit(solution)/shard_map/all_to_all | solution.py:12
  129.5 22.9 %copy-start.11 = (bf16[32,1,128,128]{3,2,0,1:T(8,128)(2,1)}, bf16[32,1,128,128]{3,2,0,1:T(8,128)(2,1)S(1)}, u32[]{:S(2)}) copy-start(bf16[32,1,128,128]{3,2,0,1:T(8,128)(2,1)S(1)} %pad_maximum_fusion.1) | copy-start | bytes 3145732
  131.0 21.4 %copy-start.26 = (bf16[32,1,128,128]{3,2,0,1:T(8,128)(2,1)}, bf16[32,1,128,128]{3,2,0,1:T(8,128)(2,1)S(1)}, u32[]{:S(2)}) copy-start(bf16[32,1,128,128]{3,2,0,1:T(8,128)(2,1)S(1)} %pad_maximum_fusion.2) | copy-start | bytes 3145732
  132.2 6.1 copy-start.17
  132.2 6.1 copy-start.32
  741.4 75.2 %all-to-all-start.8 = ((bf16[32,2,8192]{2,1,0:T(2,128)(2,1)}), bf16[32,2,8192]{2,1,0:T(2,128)(2,1)S(1)}, u32[]{:S(2)}, u32[]{:S(2)}) async-start(bf16[32,2,8192]{2,1,0:T(2,128)(2,1)} %reshape.1123), calls=%async_computation.8 | async-start | bytes 2097152 | tf_op jit(solution)/shard_map/all_to_all | solution.py:173
  774.2 9.6 slice-start
  816.6 99.3 %all-to-all-start.6 = ((bf16[32,2,8192]{2,1,0:T(2,128)(2,1)}), bf16[32,2,8192]{2,1,0:T(2,128)(2,1)}, u32[]{:S(2)}, u32[]{:S(2)}) async-start(bf16[32,2,8192]{2,1,0:T(2,128)(2,1)} %reshape.1121), calls=%async_computation.6 | async-start | bytes 2097152 | tf_op jit(solution)/shard_map/all_to_all | solution.py:162
  841.5 7.3 slice-start.8
  843.7 7.4 slice-start.6
  846.7 7.1 slice-start.4
  916.0 71.1 %all-to-all-start.9 = ((bf16[3,4096,128]{2,0,1:T(4,128)(2,1)}), bf16[3,4096,128]{2,0,1:T(4,128)(2,1)}, u32[]{:S(2)}, u32[]{:S(2)}) async-start(bf16[3,4096,128]{2,0,1:T(4,128)(2,1)} %copy.78), calls=%async_computation.9 | async-start | bytes 8388608 | tf_op jit(solution)/shard_map/all_to_all | solution.py:45
  933.3 8.1 copy-start.31
  1006.2 6.8 copy-start.1
  (32 other events, 109.4 us)
